TPU v7x, 32 devices: a whole 2x2x4 slice. The times are simulated.
32 devices in a mesh: group: 4 (over y, core), tile: 8 (over z, x).
Axes of the slice: x: 2, y: 2, z: 4, core: 2. Of those that a mesh axis runs over, the one named last changes fastest.
Arguments:
- checkpoint: float32 [16, 512, 768], P(None, ('group', 'tile')), may hold values from -6 to 6
- adjoint_in: float32 [16, 512, 768], P(None, ('group', 'tile')), may hold values from -6 to 6
- courant_x: float32 [16, 512, 768], P(None, ('group', 'tile')), may hold values from 0.05 to 0.5
- courant_y: float32 [16, 512, 768], P(None, ('group', 'tile')), may hold values from 0.05 to 0.5
- mixing: float32 [15, 512, 768], P(None, ('group', 'tile')), may hold values from 0.02 to 0.3
- snd_column: int32 [32, 8, 128], P(('group', 'tile')), may hold values from 0 to 12287
- snd_count: int32 [32, 8], P(('group', 'tile')), may hold values from 32 to 128, as said below
- snd_step: int32 [32, 8, 128], P(('group', 'tile')), may hold values from 0 to 1
- snd_value: float32 [32, 8, 128], P(('group', 'tile')), may hold values from -6 to 6
- snd_weight: float32 [32, 8, 128], P(('group', 'tile')), may hold values from 0.3 to 3
- snd_kernel: float32 [32, 8, 16, 128], P(('group', 'tile')), may hold values from 0 to 0.5
Outputs:
- adjoint_out: float32 [16, 512, 768], P(None, ('group', 'tile'))
Inputs may be any that keep to these rules, and one draw needn't show every extreme that they name: `snd_count`: at most 128; in every draw some destination tile receives 128 soundings from every source device of each group, and every source device fills all slots of some destination tile.
All inputs are finite; a program needn't handle non-finite values.
Results may differ from a plain program's by a relative error of at most 0.0001.
Values sent between devices are 32-bit elements; how exact they have to be, the bound alone decides.
A program may use at most 64 MiB of HBM per device.

v0:
```python
import jax
import jax.numpy as jnp
from jax import lax
from jax.sharding import PartitionSpec as P

STEPS = 2


def with_halo(block, sides, width):
    for axis, dim in sides:
        count = lax.axis_size(axis)
        forward = [(i, i + 1) for i in range(count - 1)]
        forward.append((count - 1, 0))
        backward = [(target, source) for source, target in forward]
        low = lax.ppermute(
            lax.slice_in_dim(block, block.shape[dim] - width, None, axis=dim), axis, forward
        )
        high = lax.ppermute(lax.slice_in_dim(block, 0, width, axis=dim), axis, backward)
        block = jnp.concatenate([low, block, high], axis=dim)
    return block


def from_behind(block, axis, distance):
    devices = range(lax.axis_size(axis))
    route = [((i - distance) % len(devices), i) for i in devices]
    return lax.ppermute(block, axis, route)


def pad_periodic(field, width, along):
    total = field.shape[along]
    return jnp.concatenate(
        [
            lax.slice_in_dim(field, total - width, total, axis=along),
            field,
            lax.slice_in_dim(field, 0, width, axis=along),
        ],
        axis=along,
    )


def sweep_forward(padded, courant_pad, along):
    interior = padded.shape[along] - 4

    def piece_of(first, last):
        return lax.slice_in_dim(padded, first, last, axis=along)

    courant_face = lax.slice_in_dim(courant_pad, 0, interior + 1, axis=along)
    fluxes = (
        courant_face
        * (
            2.0 * piece_of(2, interior + 3)
            + 5.0 * piece_of(1, interior + 2)
            - piece_of(0, interior + 1)
        )
        / 6.0
    )
    return (
        piece_of(2, interior + 2)
        + lax.slice_in_dim(fluxes, 0, interior, axis=along)
        - lax.slice_in_dim(fluxes, 1, interior + 1, axis=along)
    )


def sweep_adjoint(padded, courant_pad, along):
    interior = padded.shape[along] - 4

    def piece_of(first, last):
        return lax.slice_in_dim(padded, first, last, axis=along)

    differences = piece_of(2, interior + 4) - piece_of(1, interior + 3)
    scaled = courant_pad * differences
    return (
        piece_of(2, interior + 2)
        + (
            2.0 * lax.slice_in_dim(scaled, 0, interior, axis=along)
            + 5.0 * lax.slice_in_dim(scaled, 1, interior + 1, axis=along)
            - lax.slice_in_dim(scaled, 2, interior + 2, axis=along)
        )
        / 6.0
    )


def vertical_mix(field, mixing):
    fluxes = mixing * (field[1:] - field[:-1])
    zero_row = jnp.zeros_like(field[:1])
    return (
        field
        + jnp.concatenate([fluxes, zero_row], axis=0)
        - jnp.concatenate([zero_row, fluxes], axis=0)
    )


def horizontal(rimmed, wind_x, wind_y):
    swept = sweep_forward(rimmed, wind_x, 1)
    return sweep_forward(pad_periodic(swept, 2, 2), wind_y, 2)


def on_device(
    checkpoint,
    adjoint_in,
    courant_x,
    courant_y,
    mixing,
    snd_column,
    snd_count,
    snd_step,
    snd_value,
    snd_weight,
    snd_kernel,
):
    levels, width_x, width_y = checkpoint.shape
    tile_count = snd_column.shape[1]
    capacity = snd_column.shape[2]
    wind_x = with_halo(courant_x, ((("group", "tile"), 1),), 1)
    wind_y = pad_periodic(courant_y, 1, 2)
    tracer = from_behind(checkpoint, "group", 1)
    rimmed = with_halo(tracer, ((("group", "tile"), 1),), 2)
    tracer = vertical_mix(horizontal(rimmed, wind_x, wind_y), mixing)
    states = [tracer]
    moment = 1
    rimmed = with_halo(tracer, ((("group", "tile"), 1),), 2)
    tracer = vertical_mix(horizontal(rimmed, wind_x, wind_y), mixing)
    states.append(tracer)
    position = lax.broadcasted_iota(jnp.int32, snd_column.shape, 2)
    weight = jnp.where(position < snd_count[:, :, None], snd_weight, jnp.zeros_like(snd_weight))
    values, weights, kernels = (
        lax.all_to_all(snd_value, "tile", split_axis=1, concat_axis=0, tiled=True),
        lax.all_to_all(weight, "tile", split_axis=1, concat_axis=0, tiled=True),
        lax.all_to_all(snd_kernel, "tile", split_axis=1, concat_axis=0, tiled=True),
    )
    columns, step_ids = (
        lax.all_to_all(snd_column, "tile", split_axis=1, concat_axis=0, tiled=True),
        lax.all_to_all(snd_step, "tile", split_axis=1, concat_axis=0, tiled=True),
    )
    values = values.reshape(tile_count, capacity)
    weights = weights.reshape(tile_count, capacity)
    kernels = kernels.reshape(tile_count, levels, capacity)
    step_ids = step_ids.reshape(tile_count, capacity)
    cell_index = columns.reshape(-1)
    forcings = []
    for moment in range(STEPS):
        flattened = states[moment].reshape(levels, -1)
        picked = jnp.take(flattened, cell_index, axis=1).reshape(levels, tile_count, capacity)
        observed = jnp.einsum("ltc,tlc->tc", picked, kernels, precision=lax.Precision.HIGHEST)
        misfit = jnp.where(
            step_ids == moment, weights * (observed - values), jnp.zeros_like(observed)
        )
        contribution = jnp.einsum(
            "tlc,tc->ltc", kernels, misfit, precision=lax.Precision.HIGHEST
        ).reshape(levels, -1)
        forcing = (
            jnp.zeros((levels, width_x * width_y), jnp.float32).at[:, cell_index].add(contribution)
        )
        forcings.append(forcing.reshape(levels, width_x, width_y))
    adjoint = adjoint_in
    for moment in reversed(range(STEPS)):
        adjoint = vertical_mix(adjoint + forcings[moment], mixing)
        adjoint = sweep_adjoint(pad_periodic(adjoint, 2, 2), wind_y, 2)
        rimmed = with_halo(adjoint, ((("group", "tile"), 1),), 2)
        adjoint = sweep_adjoint(rimmed, wind_x, 1)
    return adjoint


def solution(mesh):
    return jax.shard_map(
        on_device,
        mesh=mesh,
        in_specs=(
            P(None, ("group", "tile"), None),
            P(None, ("group", "tile"), None),
            P(None, ("group", "tile"), None),
            P(None, ("group", "tile"), None),
            P(None, ("group", "tile"), None),
            P(("group", "tile"), None, None),
            P(("group", "tile"), None),
            P(("group", "tile"), None, None),
            P(("group", "tile"), None, None),
            P(("group", "tile"), None, None),
            P(("group", "tile"), None, None, None),
        ),
        out_specs=P(None, ("group", "tile"), None),
        check_vma=False,
    )
```

profile of v0, /device:TPU:0, one launch (start us, length us, event | category | flops | bytes accessed | tf_op | source)
XLA Modules:
  0.0 144.3 jit_solution(1064985473383274465)
XLA Ops:
  0.0 7.4 %all-to-all-start = ((s32[1,8,128]{2,0,1:T(1,128)}), s32[1,8,128]{2,0,1:T(1,128)S(1)}, u32[]{:S(2)}, u32[]{:S(2)}) async-start(s32[1,8,128]{2,0,1:T(1,128)} %bitcast.75), calls=%async_computation | async-start | bytes 8192 | tf_op jit(solution)/shard_map/all_to_all | solution.py:132
  13.8 5.0 %all-to-all-start.2 = ((f32[1,8,128]{2,0,1:T(1,128)}), f32[1,8,128]{2,0,1:T(1,128)S(1)}, u32[]{:S(2)}, u32[]{:S(2)}) async-start(f32[1,8,128]{2,0,1:T(1,128)} %compare_select_fusion.1), calls=%async_computation.2 | async-start | bytes 8192 | tf_op jit(solution)/shard_map/all_to_all | solution.py:128
  21.2 3.8 %collective-permute-start.2 = (f32[16,2,768]{2,1,0:T(2,128)S(1)}, f32[16,2,768]{2,1,0:T(2,128)S(1)}, u32[]{:S(2)}, u32[]{:S(2)}) collective-permute-start(f32[16,2,768]{2,1,0:T(2,128)S(1)} %get-tuple-element.26), channel_id=1, source_target_pairs={{1,0},{2,1},{3,2},{4,3},{5,4},{6,5},{7,6},{8,7},{9,8},{10,9},{11,1... | collective-permute-start | bytes 294920 | tf_op jit(solution)/shard_map/ppermute | solution.py:18
  25.1 3.3 %collective-permute-done.3 = f32[16,2,768]{2,1,0:T(2,128)S(1)} collective-permute-done((f32[16,2,768]{2,1,0:T(2,128)S(1)}, f32[16,2,768]{2,1,0:T(2,128)S(1)}, u32[]{:S(2)}, u32[]{:S(2)}) %collective-permute-start.3) | collective-permute-done | bytes 98336 | tf_op jit(solution)/shard_map/ppermute | solution.py:15
  33.0 5.3 %collective-permute-start.4 = (f32[16,2,768]{2,1,0:T(2,128)}, f32[16,2,768]{2,1,0:T(2,128)}, u32[]{:S(2)}, u32[]{:S(2)}) collective-permute-start(f32[16,2,768]{2,1,0:T(2,128)} %get-tuple-element.22), channel_id=1, source_target_pairs={{1,0},{2,1},{3,2},{4,3},{5,4},{6,5},{7,6},{8,7},{9,8},{10,9},{11,1... | collective-permute-start | bytes 294920 | tf_op jit(solution)/shard_map/ppermute | solution.py:18
  38.3 3.9 %copy.49 = f32[16,16,768]{0,2,1:T(8,128)} copy(f32[16,16,768]{2,1,0:T(8,128)S(1)} %pad_subtract_fusion.3) | data formatting | bytes 1572864 | tf_op jit(solution)/shard_map/sub | solution.py:87
  42.3 6.8 %gather_fusion.1 = f32[1024,16]{1,0:T(8,128)} fusion(f32[16,12288]{0,1:T(8,128)} %bitcast.66, s32[1024]{0:T(1024)S(1)} %fusion.53), kind=kCustom, calls=%fused_computation.1.clone | custom fusion | bytes 135168 | tf_op jit(solution)/shard_map/jit(_take)/gather | solution.py:143
  52.9 3.3 %all-to-all-start.4 = ((f32[1,8,128]{2,0,1:T(1,128)}), f32[1,8,128]{2,0,1:T(1,128)S(1)}, u32[]{:S(2)}, u32[]{:S(2)}) async-start(f32[1,8,128]{2,0,1:T(1,128)} %bitcast.22), calls=%async_computation.4 | async-start | bytes 8192 | tf_op jit(solution)/shard_map/all_to_all | solution.py:127
  56.3 2.3 %pad_subtract_fusion.2 = f32[16,16,768]{2,1,0:T(8,128)} fusion(f32[15,16,768]{2,1,0:T(8,128)} %fusion.47, f32[16,16,768]{2,1,0:T(8,128)S(1)} %slice_subtract_fusion.4), kind=kLoop, calls=%fused_computation.95 | loop fusion | flops 393216 | bytes 2310144 | tf_op jit(solution)/shard_map/sub | solution.py:87
  58.6 4.8 %copy.42 = f32[16,16,768]{0,2,1:T(8,128)} copy(f32[16,16,768]{2,1,0:T(8,128)} %pad_subtract_fusion.2) | data formatting | bytes 1572864 | tf_op jit(solution)/shard_map/sub | solution.py:87
  63.5 6.8 %gather_fusion = f32[1024,16]{1,0:T(8,128)} fusion(f32[16,12288]{0,1:T(8,128)} %bitcast.65, s32[1024]{0:T(1024)S(1)} %fusion.53), kind=kCustom, calls=%fused_computation.clone | custom fusion | bytes 135168 | tf_op jit(solution)/shard_map/jit(_take)/gather | solution.py:143
  70.3 5.9 %all-to-all-start.3 = ((f32[1,8,16,128]{3,2,0,1:T(8,128)}), f32[1,8,16,128]{3,2,0,1:T(8,128)S(1)}, u32[]{:S(2)}, u32[]{:S(2)}) async-start(f32[1,8,16,128]{3,2,0,1:T(8,128)} %bitcast.19), calls=%async_computation.3 | async-start | bytes 131072 | tf_op jit(solution)/shard_map/all_to_all | solution.py:129
  76.2 2.2 %broadcast_select_fusion = (f32[1024,16]{1,0:T(8,128)S(1)}, f32[1024,16]{1,0:T(8,128)}) fusion(f32[1024,16]{1,0:T(8,128)} %gather_fusion.1, pred[1024]{0:T(1024)(128)(4,1)S(1)} %compare_and_fusion, f32[1024,16]{1,0:T(8,128)} %gather_fusion), kind=kLoop, calls=%fused_computation.105 | loop fusion | flops 32768 | bytes 263168 | tf_op jit(solution)/shard_map/jit(_take)/select_n | solution.py:143
  79.8 3.3 %all-to-all-done.3 = f32[1,8,16,128]{3,2,0,1:T(8,128)S(1)} async-done(((f32[1,8,16,128]{3,2,0,1:T(8,128)}), f32[1,8,16,128]{3,2,0,1:T(8,128)S(1)}, u32[]{:S(2)}, u32[]{:S(2)}) %all-to-all-start.3) | async-done | bytes 65568 | tf_op jit(solution)/shard_map/all_to_all | solution.py:129
  83.1 3.3 %all-to-all-start.1 = ((s32[1,8,128]{2,0,1:T(1,128)}), s32[1,8,128]{2,0,1:T(1,128)S(1)}, u32[]{:S(2)}, u32[]{:S(2)}) async-start(s32[1,8,128]{2,0,1:T(1,128)} %bitcast.7), calls=%async_computation.1 | async-start | bytes 8192 | tf_op jit(solution)/shard_map/all_to_all | solution.py:133
  86.5 6.3 %all-to-all-done.1 = s32[1,8,128]{2,0,1:T(1,128)S(1)} async-done(((s32[1,8,128]{2,0,1:T(1,128)}), s32[1,8,128]{2,0,1:T(1,128)S(1)}, u32[]{:S(2)}, u32[]{:S(2)}) %all-to-all-start.1) | async-done | bytes 4128 | tf_op jit(solution)/shard_map/all_to_all | solution.py:133
  93.0 9.0 %scatter_custom_fusion = f32[16,12288]{0,1:T(8,128)} fusion(s32[1024]{0:T(1024)S(1)} %bitcast.76, f32[1024,16]{1,0:T(8,128)S(1)} %copy.46, f32[]{:T(128)} %constant.15.clone.1), kind=kCustom, calls=%fused_computation.6 | custom fusion | flops 16384 | bytes 786436 | tf_op jit(solution)/shard_map/scatter-add | solution.py:152
  102.1 4.5 %copy.47 = f32[16,16,768]{2,1,0:T(8,128)S(1)} copy(f32[16,16,768]{0,2,1:T(8,128)} %bitcast.64) | data formatting | bytes 1572864 | tf_op jit(solution)/shard_map/reshape | solution.py:154
  109.9 2.0 %collective-permute-start.8 = (f32[16,2,768]{2,1,0:T(2,128)}, f32[16,2,768]{2,1,0:T(2,128)}, u32[]{:S(2)}, u32[]{:S(2)}) collective-permute-start(f32[16,2,768]{2,1,0:T(2,128)} %get-tuple-element.14), channel_id=1, source_target_pairs={{0,1},{1,2},{2,3},{3,4},{4,5},{5,6},{6,7},{7,8},{8,9},{9,10},{10,1... | collective-permute-start | bytes 294920 | tf_op jit(solution)/shard_map/ppermute | solution.py:15
  111.9 3.3 %collective-permute-start.6 = (f32[16,1,768]{2,1,0:T(1,128)}, f32[16,1,768]{2,1,0:T(1,128)S(1)}, u32[]{:S(2)}, u32[]{:S(2)}) collective-permute-start(f32[16,1,768]{2,1,0:T(1,128)} %get-tuple-element.12), channel_id=1, source_target_pairs={{1,0},{2,1},{3,2},{4,3},{5,4},{6,5},{7,6},{8,7},{9,8},{10,9},{11,1... | collective-permute-start | bytes 147464 | tf_op jit(solution)/shard_map/ppermute | solution.py:18
  116.3 9.4 %scatter_custom_fusion.1 = f32[16,12288]{0,1:T(8,128)} fusion(s32[1024]{0:T(1024)S(1)} %bitcast.77, f32[1024,16]{1,0:T(8,128)} %copy.51, f32[]{:T(128)} %constant.15.clone.1), kind=kCustom, calls=%fused_computation.4 | custom fusion | flops 16384 | bytes 786944 | tf_op jit(solution)/shard_map/scatter-add | solution.py:152
  125.7 5.3 %copy.52 = f32[16,16,768]{2,1,0:T(8,128)} copy(f32[16,16,768]{0,2,1:T(8,128)} %bitcast.63) | data formatting | bytes 1572864 | tf_op jit(solution)/shard_map/reshape | solution.py:154
  136.4 2.6 %collective-permute-done.9 = f32[16,2,768]{2,1,0:T(2,128)S(1)} collective-permute-done((f32[16,2,768]{2,1,0:T(2,128)S(1)}, f32[16,2,768]{2,1,0:T(2,128)S(1)}, u32[]{:S(2)}, u32[]{:S(2)}) %collective-permute-start.9) | collective-permute-done | bytes 98336 | tf_op jit(solution)/shard_map/ppermute | solution.py:18
  139.0 3.7 %collective-permute-done.10 = f32[16,2,768]{2,1,0:T(2,128)S(1)} collective-permute-done((f32[16,2,768]{2,1,0:T(2,128)S(1)}, f32[16,2,768]{2,1,0:T(2,128)S(1)}, u32[]{:S(2)}, u32[]{:S(2)}) %collective-permute-start.10) | collective-permute-done | bytes 98336 | tf_op jit(solution)/shard_map/ppermute | solution.py:15
  (72 shorter events, 30.0 us)
Async XLA Ops:
  0.0 28.4 %copy-start.1 = (f32[16,16,768]{2,1,0:T(8,128)S(1)}, f32[16,16,768]{2,1,0:T(8,128)}, u32[]{:S(2)}) copy-start(f32[16,16,768]{2,1,0:T(8,128)} %param.15) | copy-start | bytes 2359300
  0.0 13.8 %all-to-all-start = ((s32[1,8,128]{2,0,1:T(1,128)}), s32[1,8,128]{2,0,1:T(1,128)S(1)}, u32[]{:S(2)}, u32[]{:S(2)}) async-start(s32[1,8,128]{2,0,1:T(1,128)} %bitcast.75), calls=%async_computation | async-start | bytes 8192 | tf_op jit(solution)/shard_map/all_to_all | solution.py:132
  7.4 12.2 %collective-permute-start = (f32[16,16,768]{2,1,0:T(8,128)}, f32[16,16,768]{2,1,0:T(8,128)S(1)}, u32[]{:S(2)}, u32[]{:S(2)}) collective-permute-start(f32[16,16,768]{2,1,0:T(8,128)} %param.13), channel_id=1, source_target_pairs={{24,0},{0,8},{8,16},{16,24},{25,1},{1,9},{9,17},{17,25},{26,2},{2,... | collective-permute-start | bytes 2359304 | tf_op jit(solution)/shard_map/ppermute | solution.py:26
  9.2 15.8 %collective-permute-start.1 = (f32[16,1,768]{2,1,0:T(1,128)S(1)}, f32[16,1,768]{2,1,0:T(1,128)S(1)}, u32[]{:S(2)}, u32[]{:S(2)}) collective-permute-start(f32[16,1,768]{2,1,0:T(1,128)S(1)} %get-tuple-element.13), channel_id=1, source_target_pairs={{0,1},{1,2},{2,3},{3,4},{4,5},{5,6},{6,7},{7,8},{8,9},{9,10},{10,1... | collective-permute-start | bytes 147464 | tf_op jit(solution)/shard_map/ppermute | solution.py:15
  13.8 39.1 %all-to-all-start.2 = ((f32[1,8,128]{2,0,1:T(1,128)}), f32[1,8,128]{2,0,1:T(1,128)S(1)}, u32[]{:S(2)}, u32[]{:S(2)}) async-start(f32[1,8,128]{2,0,1:T(1,128)} %compare_select_fusion.1), calls=%async_computation.2 | async-start | bytes 8192 | tf_op jit(solution)/shard_map/all_to_all | solution.py:128
  19.6 8.7 %collective-permute-start.3 = (f32[16,2,768]{2,1,0:T(2,128)S(1)}, f32[16,2,768]{2,1,0:T(2,128)S(1)}, u32[]{:S(2)}, u32[]{:S(2)}) collective-permute-start(f32[16,2,768]{2,1,0:T(2,128)S(1)} %get-tuple-element.27), channel_id=1, source_target_pairs={{0,1},{1,2},{2,3},{3,4},{4,5},{5,6},{6,7},{7,8},{8,9},{9,10},{10,1... | collective-permute-start | bytes 294920 | tf_op jit(solution)/shard_map/ppermute | solution.py:15
  21.2 7.2 %collective-permute-start.2 = (f32[16,2,768]{2,1,0:T(2,128)S(1)}, f32[16,2,768]{2,1,0:T(2,128)S(1)}, u32[]{:S(2)}, u32[]{:S(2)}) collective-permute-start(f32[16,2,768]{2,1,0:T(2,128)S(1)} %get-tuple-element.26), channel_id=1, source_target_pairs={{1,0},{2,1},{3,2},{4,3},{5,4},{6,5},{7,6},{8,7},{9,8},{10,9},{11,1... | collective-permute-start | bytes 294920 | tf_op jit(solution)/shard_map/ppermute | solution.py:18
  29.0 1.1 copy-start
  30.9 1.1 copy-start.2
  33.0 16.1 %collective-permute-start.5 = (f32[16,2,768]{2,1,0:T(2,128)}, f32[16,2,768]{2,1,0:T(2,128)S(1)}, u32[]{:S(2)}, u32[]{:S(2)}) collective-permute-start(f32[16,2,768]{2,1,0:T(2,128)} %get-tuple-element.23), channel_id=1, source_target_pairs={{0,1},{1,2},{2,3},{3,4},{4,5},{5,6},{6,7},{7,8},{8,9},{9,10},{10,1... | collective-permute-start | bytes 294920 | tf_op jit(solution)/shard_map/ppermute | solution.py:15
  33.0 16.1 %collective-permute-start.4 = (f32[16,2,768]{2,1,0:T(2,128)}, f32[16,2,768]{2,1,0:T(2,128)}, u32[]{:S(2)}, u32[]{:S(2)}) collective-permute-start(f32[16,2,768]{2,1,0:T(2,128)} %get-tuple-element.22), channel_id=1, source_target_pairs={{1,0},{2,1},{3,2},{4,3},{5,4},{6,5},{7,6},{8,7},{9,8},{10,9},{11,1... | collective-permute-start | bytes 294920 | tf_op jit(solution)/shard_map/ppermute | solution.py:18
  52.9 17.3 %all-to-all-start.4 = ((f32[1,8,128]{2,0,1:T(1,128)}), f32[1,8,128]{2,0,1:T(1,128)S(1)}, u32[]{:S(2)}, u32[]{:S(2)}) async-start(f32[1,8,128]{2,0,1:T(1,128)} %bitcast.22), calls=%async_computation.4 | async-start | bytes 8192 | tf_op jit(solution)/shard_map/all_to_all | solution.py:127
  70.3 12.8 %all-to-all-start.3 = ((f32[1,8,16,128]{3,2,0,1:T(8,128)}), f32[1,8,16,128]{3,2,0,1:T(8,128)S(1)}, u32[]{:S(2)}, u32[]{:S(2)}) async-start(f32[1,8,16,128]{3,2,0,1:T(8,128)} %bitcast.19), calls=%async_computation.3 | async-start | bytes 131072 | tf_op jit(solution)/shard_map/all_to_all | solution.py:129
  83.1 9.7 %all-to-all-start.1 = ((s32[1,8,128]{2,0,1:T(1,128)}), s32[1,8,128]{2,0,1:T(1,128)S(1)}, u32[]{:S(2)}, u32[]{:S(2)}) async-start(s32[1,8,128]{2,0,1:T(1,128)} %bitcast.7), calls=%async_computation.1 | async-start | bytes 8192 | tf_op jit(solution)/shard_map/all_to_all | solution.py:133
  109.9 21.1 %collective-permute-start.7 = (f32[16,2,768]{2,1,0:T(2,128)}, f32[16,2,768]{2,1,0:T(2,128)}, u32[]{:S(2)}, u32[]{:S(2)}) collective-permute-start(f32[16,2,768]{2,1,0:T(2,128)} %get-tuple-element.15), channel_id=1, source_target_pairs={{1,0},{2,1},{3,2},{4,3},{5,4},{6,5},{7,6},{8,7},{9,8},{10,9},{11,1... | collective-permute-start | bytes 294920 | tf_op jit(solution)/shard_map/ppermute | solution.py:18
  109.9 21.1 %collective-permute-start.8 = (f32[16,2,768]{2,1,0:T(2,128)}, f32[16,2,768]{2,1,0:T(2,128)}, u32[]{:S(2)}, u32[]{:S(2)}) collective-permute-start(f32[16,2,768]{2,1,0:T(2,128)} %get-tuple-element.14), channel_id=1, source_target_pairs={{0,1},{1,2},{2,3},{3,4},{4,5},{5,6},{6,7},{7,8},{8,9},{9,10},{10,1... | collective-permute-start | bytes 294920 | tf_op jit(solution)/shard_map/ppermute | solution.py:15
  111.9 19.1 %collective-permute-start.6 = (f32[16,1,768]{2,1,0:T(1,128)}, f32[16,1,768]{2,1,0:T(1,128)S(1)}, u32[]{:S(2)}, u32[]{:S(2)}) collective-permute-start(f32[16,1,768]{2,1,0:T(1,128)} %get-tuple-element.12), channel_id=1, source_target_pairs={{1,0},{2,1},{3,2},{4,3},{5,4},{6,5},{7,6},{8,7},{9,8},{10,9},{11,1... | collective-permute-start | bytes 147464 | tf_op jit(solution)/shard_map/ppermute | solution.py:18
  131.0 1.5 %copy-start.3 = (f32[16,16,768]{2,1,0:T(8,128)S(1)}, f32[16,16,768]{2,1,0:T(8,128)}, u32[]{:S(2)}) copy-start(f32[16,16,768]{2,1,0:T(8,128)} %copy.52) | copy-start | bytes 2359300
  134.3 4.7 %collective-permute-start.9 = (f32[16,2,768]{2,1,0:T(2,128)S(1)}, f32[16,2,768]{2,1,0:T(2,128)S(1)}, u32[]{:S(2)}, u32[]{:S(2)}) collective-permute-start(f32[16,2,768]{2,1,0:T(2,128)S(1)} %get-tuple-element.9), channel_id=1, source_target_pairs={{1,0},{2,1},{3,2},{4,3},{5,4},{6,5},{7,6},{8,7},{9,8},{10,9},{11,1... | collective-permute-start | bytes 294920 | tf_op jit(solution)/shard_map/ppermute | solution.py:18
  134.4 8.3 %collective-permute-start.10 = (f32[16,2,768]{2,1,0:T(2,128)S(1)}, f32[16,2,768]{2,1,0:T(2,128)S(1)}, u32[]{:S(2)}, u32[]{:S(2)}) collective-permute-start(f32[16,2,768]{2,1,0:T(2,128)S(1)} %get-tuple-element.8), channel_id=1, source_target_pairs={{0,1},{1,2},{2,3},{3,4},{4,5},{5,6},{6,7},{7,8},{8,9},{9,10},{10,1... | collective-permute-start | bytes 294920 | tf_op jit(solution)/shard_map/ppermute | solution.py:15
where the time goes:
time: 145 us; the launch traced here: 144 us
  starting transfers between devices  45.2 us (31%)
  local copies, waits for them, and re-layouts  41.3 us (28%)
  other arithmetic  37.4 us (26%)
  waiting for transfers between devices  20.1 us (14%)
    scatter-add x2, other arithmetic, on_device(): jnp.zeros((levels, width_x * width_y), jnp.float32).at[:, cell_index]  18.4 us
    gather x2, local copies, waits for them, and re-layouts, on_device(): jnp.take(flattened, cell_index, axis=1)  13.6 us
    ppermute x5, starting transfers between devices, with_halo(): lax.ppermute(lax.slice_in_dim(block, 0, width, axis=dim), axis, backward)  12.6 us
    reshape x2, local copies, waits for them, and re-layouts, on_device(): forcings.append(forcing.reshape(levels, width_x, width_y))  9.79 us
    sub x2, local copies, waits for them, and re-layouts, vertical_mix(): field + jnp.concatenate([fluxes, zero_row], axis=0)  8.8 us
    ppermute x5, starting transfers between devices, with_halo(): lax.ppermute(lax.slice_in_dim(block, block.shape[dim] - width, None, axis...  7.6 us
    all_to_all x1, starting transfers between devices, on_device(): lax.all_to_all(snd_column, 'tile', split_axis=1, concat_axis=0, tiled=True)  7.41 us
    ppermute x5, waiting for transfers between devices, with_halo(): lax.ppermute(lax.slice_in_dim(block, block.shape[dim] - width, None, axis...  7 us
  transfers between devices with their start and end apart: 16, of which 7 were waited for; matrix products, arithmetic and copies ran while one was open for 38% of the time, Pallas kernels for 0%

commit v1 on v0

--- a/solution.py
+++ b/solution.py
@@ -126,7 +126,12 @@
     values, weights, kernels = (
         lax.all_to_all(snd_value, "tile", split_axis=1, concat_axis=0, tiled=True),
         lax.all_to_all(weight, "tile", split_axis=1, concat_axis=0, tiled=True),
-        lax.all_to_all(snd_kernel, "tile", split_axis=1, concat_axis=0, tiled=True),
+        jnp.concatenate(
+            lax.all_to_all(
+                jnp.stack(jnp.split(snd_kernel, lax.axis_size("tile"), axis=1)), "tile", 0, 0
+            ),
+            axis=0,
+        ),
     )
     columns, step_ids = (
         lax.all_to_all(snd_column, "tile", split_axis=1, concat_axis=0, tiled=True),

time: 145 us -> 155 us (1.069)
  local copies, waits for them, and re-layouts: 41.3 us -> 51.6 us
    unnamed x10 -> x17, local copies, waits for them, and re-layouts: 3 us -> 12 us
  transfers between devices with their start and end apart: 16 -> 16, of which waited for: 7 -> 5; matrix products, arithmetic and copies ran while one was open for 38% -> 43% of each run, Pallas kernels for 0% -> 0%
where the time goes in v1:
time: 155 us; the launch traced here: 154 us
  local copies, waits for them, and re-layouts  51.6 us (33%)
  starting transfers between devices  45.4 us (29%)
  other arithmetic  37.4 us (24%)
  waiting for transfers between devices  19.1 us (12%)
    scatter-add x2, other arithmetic, on_device(): jnp.zeros((levels, width_x * width_y), jnp.float32).at[:, cell_index]  18.4 us
    gather x2, local copies, waits for them, and re-layouts, on_device(): jnp.take(flattened, cell_index, axis=1)  13.6 us
    unnamed x17, local copies, waits for them, and re-layouts  12 us
    ppermute x5, starting transfers between devices, with_halo(): lax.ppermute(lax.slice_in_dim(block, 0, width, axis=dim), axis, backward)  11.8 us
    reshape x2, local copies, waits for them, and re-layouts, on_device(): forcings.append(forcing.reshape(levels, width_x, width_y))  9.79 us
    sub x2, local copies, waits for them, and re-layouts, vertical_mix(): field + jnp.concatenate([fluxes, zero_row], axis=0)  8.8 us
    ppermute x5, starting transfers between devices, with_halo(): lax.ppermute(lax.slice_in_dim(block, block.shape[dim] - width, None, axis...  8.37 us
    all_to_all x1, starting transfers between devices, on_device(): lax.all_to_all(snd_column, 'tile', split_axis=1, concat_axis=0, tiled=True)  7.41 us
  transfers between devices with their start and end apart: 16, of which 5 were waited for; matrix products, arithmetic and copies ran while one was open for 43% of the time, Pallas kernels for 0%

profile of v1, /device:TPU:0, one launch (start us, length us, event | category | flops | bytes accessed | tf_op | source)
XLA Modules:
  0.0 153.8 jit_solution(2586987029472524530)
XLA Ops:
  0.0 7.4 %all-to-all-start = ((s32[1,8,128]{2,0,1:T(1,128)}), s32[1,8,128]{2,0,1:T(1,128)S(1)}, u32[]{:S(2)}, u32[]{:S(2)}) async-start(s32[1,8,128]{2,0,1:T(1,128)} %bitcast.90), calls=%async_computation | async-start | bytes 8192 | tf_op jit(solution)/shard_map/all_to_all | solution.py:137
  24.0 5.2 %all-to-all-start.2 = ((f32[1,8,128]{2,0,1:T(1,128)}), f32[1,8,128]{2,0,1:T(1,128)S(1)}, u32[]{:S(2)}, u32[]{:S(2)}) async-start(f32[1,8,128]{2,0,1:T(1,128)} %compare_select_fusion.1), calls=%async_computation.2 | async-start | bytes 8192 | tf_op jit(solution)/shard_map/all_to_all | solution.py:128
  29.3 2.1 %collective-permute-start.3 = (f32[16,2,768]{2,1,0:T(2,128)S(1)}, f32[16,2,768]{2,1,0:T(2,128)S(1)}, u32[]{:S(2)}, u32[]{:S(2)}) collective-permute-start(f32[16,2,768]{2,1,0:T(2,128)S(1)} %get-tuple-element.27), channel_id=1, source_target_pairs={{0,1},{1,2},{2,3},{3,4},{4,5},{5,6},{6,7},{7,8},{8,9},{9,10},{10,1... | collective-permute-start | bytes 294920 | tf_op jit(solution)/shard_map/ppermute | solution.py:15
  31.4 3.3 %collective-permute-start.2 = (f32[16,2,768]{2,1,0:T(2,128)S(1)}, f32[16,2,768]{2,1,0:T(2,128)S(1)}, u32[]{:S(2)}, u32[]{:S(2)}) collective-permute-start(f32[16,2,768]{2,1,0:T(2,128)S(1)} %get-tuple-element.26), channel_id=1, source_target_pairs={{1,0},{2,1},{3,2},{4,3},{5,4},{6,5},{7,6},{8,7},{9,8},{10,9},{11,1... | collective-permute-start | bytes 294920 | tf_op jit(solution)/shard_map/ppermute | solution.py:18
  34.7 3.4 %collective-permute-done.3 = f32[16,2,768]{2,1,0:T(2,128)S(1)} collective-permute-done((f32[16,2,768]{2,1,0:T(2,128)S(1)}, f32[16,2,768]{2,1,0:T(2,128)S(1)}, u32[]{:S(2)}, u32[]{:S(2)}) %collective-permute-start.3) | collective-permute-done | bytes 98336 | tf_op jit(solution)/shard_map/ppermute | solution.py:15
  43.0 5.1 %collective-permute-start.4 = (f32[16,2,768]{2,1,0:T(2,128)}, f32[16,2,768]{2,1,0:T(2,128)}, u32[]{:S(2)}, u32[]{:S(2)}) collective-permute-start(f32[16,2,768]{2,1,0:T(2,128)} %get-tuple-element.22), channel_id=1, source_target_pairs={{1,0},{2,1},{3,2},{4,3},{5,4},{6,5},{7,6},{8,7},{9,8},{10,9},{11,1... | collective-permute-start | bytes 294920 | tf_op jit(solution)/shard_map/ppermute | solution.py:18
  48.1 3.9 %copy.47 = f32[16,16,768]{0,2,1:T(8,128)} copy(f32[16,16,768]{2,1,0:T(8,128)S(1)} %pad_subtract_fusion.3) | data formatting | bytes 1572864 | tf_op jit(solution)/shard_map/sub | solution.py:87
  52.0 6.8 %gather_fusion.1 = f32[1024,16]{1,0:T(8,128)} fusion(f32[16,12288]{0,1:T(8,128)} %bitcast.81, s32[1024]{0:T(1024)S(1)} %fusion.53), kind=kCustom, calls=%fused_computation.1.clone | custom fusion | bytes 135168 | tf_op jit(solution)/shard_map/jit(_take)/gather | solution.py:148
  62.7 3.3 %all-to-all-start.4 = ((f32[1,8,128]{2,0,1:T(1,128)}), f32[1,8,128]{2,0,1:T(1,128)S(1)}, u32[]{:S(2)}, u32[]{:S(2)}) async-start(f32[1,8,128]{2,0,1:T(1,128)} %bitcast.29), calls=%async_computation.4 | async-start | bytes 8192 | tf_op jit(solution)/shard_map/all_to_all | solution.py:127
  66.0 2.3 %pad_subtract_fusion.2 = f32[16,16,768]{2,1,0:T(8,128)} fusion(f32[15,16,768]{2,1,0:T(8,128)} %fusion.47, f32[16,16,768]{2,1,0:T(8,128)S(1)} %slice_subtract_fusion.4), kind=kLoop, calls=%fused_computation.95 | loop fusion | flops 393216 | bytes 2310144 | tf_op jit(solution)/shard_map/sub | solution.py:87
  68.4 4.8 %copy.41 = f32[16,16,768]{0,2,1:T(8,128)} copy(f32[16,16,768]{2,1,0:T(8,128)} %pad_subtract_fusion.2) | data formatting | bytes 1572864 | tf_op jit(solution)/shard_map/sub | solution.py:87
  73.2 6.8 %gather_fusion = f32[1024,16]{1,0:T(8,128)} fusion(f32[16,12288]{0,1:T(8,128)} %bitcast.80, s32[1024]{0:T(1024)S(1)} %fusion.53), kind=kCustom, calls=%fused_computation.clone | custom fusion | bytes 135168 | tf_op jit(solution)/shard_map/jit(_take)/gather | solution.py:148
  80.0 5.9 %all-to-all-start.3 = ((f32[8,1,1,16,128]{4,3,2,1,0:T(8,128)}), f32[8,1,1,16,128]{4,3,2,1,0:T(8,128)S(1)}, u32[]{:S(2)}, u32[]{:S(2)}) async-start(f32[8,1,1,16,128]{4,3,2,1,0:T(8,128)} %constant_dynamic-update-slice_fusion), calls=%async_computation.3 | async-start | bytes 131072 | tf_op jit(solution)/shard_map/all_to_all | solution.py:130
  86.0 2.2 %broadcast_select_fusion = (f32[1024,16]{1,0:T(8,128)S(1)}, f32[1024,16]{1,0:T(8,128)}) fusion(f32[1024,16]{1,0:T(8,128)} %gather_fusion.1, pred[1024]{0:T(1024)(128)(4,1)S(1)} %compare_and_fusion, f32[1024,16]{1,0:T(8,128)} %gather_fusion), kind=kLoop, calls=%fused_computation.105 | loop fusion | flops 32768 | bytes 263168 | tf_op jit(solution)/shard_map/jit(_take)/select_n | solution.py:148
  89.5 3.3 %all-to-all-done.3 = f32[8,1,1,16,128]{4,3,2,1,0:T(8,128)S(1)} async-done(((f32[8,1,1,16,128]{4,3,2,1,0:T(8,128)}), f32[8,1,1,16,128]{4,3,2,1,0:T(8,128)S(1)}, u32[]{:S(2)}, u32[]{:S(2)}) %all-to-all-start.3) | async-done | bytes 65568 | tf_op jit(solution)/shard_map/all_to_all | solution.py:130
  92.9 3.3 %all-to-all-start.1 = ((s32[1,8,128]{2,0,1:T(1,128)}), s32[1,8,128]{2,0,1:T(1,128)S(1)}, u32[]{:S(2)}, u32[]{:S(2)}) async-start(s32[1,8,128]{2,0,1:T(1,128)} %bitcast.7), calls=%async_computation.1 | async-start | bytes 8192 | tf_op jit(solution)/shard_map/all_to_all | solution.py:138
  96.2 6.3 %all-to-all-done.1 = s32[1,8,128]{2,0,1:T(1,128)S(1)} async-done(((s32[1,8,128]{2,0,1:T(1,128)}), s32[1,8,128]{2,0,1:T(1,128)S(1)}, u32[]{:S(2)}, u32[]{:S(2)}) %all-to-all-start.1) | async-done | bytes 4128 | tf_op jit(solution)/shard_map/all_to_all | solution.py:138
  102.8 9.0 %scatter_custom_fusion = f32[16,12288]{0,1:T(8,128)} fusion(s32[1024]{0:T(1024)S(1)} %bitcast.91, f32[1024,16]{1,0:T(8,128)S(1)} %copy.44, f32[]{:T(128)} %constant.15.clone.1), kind=kCustom, calls=%fused_computation.6 | custom fusion | flops 16384 | bytes 786436 | tf_op jit(solution)/shard_map/scatter-add | solution.py:157
  111.8 4.5 %copy.45 = f32[16,16,768]{2,1,0:T(8,128)S(1)} copy(f32[16,16,768]{0,2,1:T(8,128)} %bitcast.79) | data formatting | bytes 1572864 | tf_op jit(solution)/shard_map/reshape | solution.py:159
  121.7 3.3 %collective-permute-start.6 = (f32[16,1,768]{2,1,0:T(1,128)}, f32[16,1,768]{2,1,0:T(1,128)S(1)}, u32[]{:S(2)}, u32[]{:S(2)}) collective-permute-start(f32[16,1,768]{2,1,0:T(1,128)} %get-tuple-element.12), channel_id=1, source_target_pairs={{1,0},{2,1},{3,2},{4,3},{5,4},{6,5},{7,6},{8,7},{9,8},{10,9},{11,1... | collective-permute-start | bytes 147464 | tf_op jit(solution)/shard_map/ppermute | solution.py:18
  126.0 9.4 %scatter_custom_fusion.1 = f32[16,12288]{0,1:T(8,128)} fusion(s32[1024]{0:T(1024)S(1)} %bitcast.92, f32[1024,16]{1,0:T(8,128)} %copy.49, f32[]{:T(128)} %constant.15.clone.1), kind=kCustom, calls=%fused_computation.4 | custom fusion | flops 16384 | bytes 786944 | tf_op jit(solution)/shard_map/scatter-add | solution.py:157
  135.4 5.3 %copy.50 = f32[16,16,768]{2,1,0:T(8,128)} copy(f32[16,16,768]{0,2,1:T(8,128)} %bitcast.78) | data formatting | bytes 1572864 | tf_op jit(solution)/shard_map/reshape | solution.py:159
  146.2 2.6 %collective-permute-done.9 = f32[16,2,768]{2,1,0:T(2,128)S(1)} collective-permute-done((f32[16,2,768]{2,1,0:T(2,128)S(1)}, f32[16,2,768]{2,1,0:T(2,128)S(1)}, u32[]{:S(2)}, u32[]{:S(2)}) %collective-permute-start.9) | collective-permute-done | bytes 98336 | tf_op jit(solution)/shard_map/ppermute | solution.py:18
  148.8 3.5 %collective-permute-done.10 = f32[16,2,768]{2,1,0:T(2,128)S(1)} collective-permute-done((f32[16,2,768]{2,1,0:T(2,128)S(1)}, f32[16,2,768]{2,1,0:T(2,128)S(1)}, u32[]{:S(2)}, u32[]{:S(2)}) %collective-permute-start.10) | collective-permute-done | bytes 98336 | tf_op jit(solution)/shard_map/ppermute | solution.py:15
  (80 shorter events, 40.3 us)
Async XLA Ops:
  0.0 38.1 %copy-start.1 = (f32[16,16,768]{2,1,0:T(8,128)S(1)}, f32[16,16,768]{2,1,0:T(8,128)}, u32[]{:S(2)}) copy-start(f32[16,16,768]{2,1,0:T(8,128)} %param.15) | copy-start | bytes 2359300
  0.0 24.0 %all-to-all-start = ((s32[1,8,128]{2,0,1:T(1,128)}), s32[1,8,128]{2,0,1:T(1,128)S(1)}, u32[]{:S(2)}, u32[]{:S(2)}) async-start(s32[1,8,128]{2,0,1:T(1,128)} %bitcast.90), calls=%async_computation | async-start | bytes 8192 | tf_op jit(solution)/shard_map/all_to_all | solution.py:137
  7.4 21.8 %collective-permute-start = (f32[16,16,768]{2,1,0:T(8,128)}, f32[16,16,768]{2,1,0:T(8,128)S(1)}, u32[]{:S(2)}, u32[]{:S(2)}) collective-permute-start(f32[16,16,768]{2,1,0:T(8,128)} %param.13), channel_id=1, source_target_pairs={{24,0},{0,8},{8,16},{16,24},{25,1},{1,9},{9,17},{17,25},{26,2},{2,... | collective-permute-start | bytes 2359304 | tf_op jit(solution)/shard_map/ppermute | solution.py:26
  9.2 25.5 %collective-permute-start.1 = (f32[16,1,768]{2,1,0:T(1,128)S(1)}, f32[16,1,768]{2,1,0:T(1,128)S(1)}, u32[]{:S(2)}, u32[]{:S(2)}) collective-permute-start(f32[16,1,768]{2,1,0:T(1,128)S(1)} %get-tuple-element.13), channel_id=1, source_target_pairs={{0,1},{1,2},{2,3},{3,4},{4,5},{5,6},{6,7},{7,8},{8,9},{9,10},{10,1... | collective-permute-start | bytes 147464 | tf_op jit(solution)/shard_map/ppermute | solution.py:15
  24.0 38.7 %all-to-all-start.2 = ((f32[1,8,128]{2,0,1:T(1,128)}), f32[1,8,128]{2,0,1:T(1,128)S(1)}, u32[]{:S(2)}, u32[]{:S(2)}) async-start(f32[1,8,128]{2,0,1:T(1,128)} %compare_select_fusion.1), calls=%async_computation.2 | async-start | bytes 8192 | tf_op jit(solution)/shard_map/all_to_all | solution.py:128
  29.3 8.8 %collective-permute-start.3 = (f32[16,2,768]{2,1,0:T(2,128)S(1)}, f32[16,2,768]{2,1,0:T(2,128)S(1)}, u32[]{:S(2)}, u32[]{:S(2)}) collective-permute-start(f32[16,2,768]{2,1,0:T(2,128)S(1)} %get-tuple-element.27), channel_id=1, source_target_pairs={{0,1},{1,2},{2,3},{3,4},{4,5},{5,6},{6,7},{7,8},{8,9},{9,10},{10,1... | collective-permute-start | bytes 294920 | tf_op jit(solution)/shard_map/ppermute | solution.py:15
  31.4 6.7 %collective-permute-start.2 = (f32[16,2,768]{2,1,0:T(2,128)S(1)}, f32[16,2,768]{2,1,0:T(2,128)S(1)}, u32[]{:S(2)}, u32[]{:S(2)}) collective-permute-start(f32[16,2,768]{2,1,0:T(2,128)S(1)} %get-tuple-element.26), channel_id=1, source_target_pairs={{1,0},{2,1},{3,2},{4,3},{5,4},{6,5},{7,6},{8,7},{9,8},{10,9},{11,1... | collective-permute-start | bytes 294920 | tf_op jit(solution)/shard_map/ppermute | solution.py:18
  38.7 1.1 copy-start
  40.7 1.1 copy-start.2
  42.7 16.1 %collective-permute-start.5 = (f32[16,2,768]{2,1,0:T(2,128)}, f32[16,2,768]{2,1,0:T(2,128)S(1)}, u32[]{:S(2)}, u32[]{:S(2)}) collective-permute-start(f32[16,2,768]{2,1,0:T(2,128)} %get-tuple-element.23), channel_id=1, source_target_pairs={{0,1},{1,2},{2,3},{3,4},{4,5},{5,6},{6,7},{7,8},{8,9},{9,10},{10,1... | collective-permute-start | bytes 294920 | tf_op jit(solution)/shard_map/ppermute | solution.py:15
  43.0 15.9 %collective-permute-start.4 = (f32[16,2,768]{2,1,0:T(2,128)}, f32[16,2,768]{2,1,0:T(2,128)}, u32[]{:S(2)}, u32[]{:S(2)}) collective-permute-start(f32[16,2,768]{2,1,0:T(2,128)} %get-tuple-element.22), channel_id=1, source_target_pairs={{1,0},{2,1},{3,2},{4,3},{5,4},{6,5},{7,6},{8,7},{9,8},{10,9},{11,1... | collective-permute-start | bytes 294920 | tf_op jit(solution)/shard_map/ppermute | solution.py:18
  62.7 17.3 %all-to-all-start.4 = ((f32[1,8,128]{2,0,1:T(1,128)}), f32[1,8,128]{2,0,1:T(1,128)S(1)}, u32[]{:S(2)}, u32[]{:S(2)}) async-start(f32[1,8,128]{2,0,1:T(1,128)} %bitcast.29), calls=%async_computation.4 | async-start | bytes 8192 | tf_op jit(solution)/shard_map/all_to_all | solution.py:127
  80.0 12.8 %all-to-all-start.3 = ((f32[8,1,1,16,128]{4,3,2,1,0:T(8,128)}), f32[8,1,1,16,128]{4,3,2,1,0:T(8,128)S(1)}, u32[]{:S(2)}, u32[]{:S(2)}) async-start(f32[8,1,1,16,128]{4,3,2,1,0:T(8,128)} %constant_dynamic-update-slice_fusion), calls=%async_computation.3 | async-start | bytes 131072 | tf_op jit(solution)/shard_map/all_to_all | solution.py:130
  92.9 9.7 %all-to-all-start.1 = ((s32[1,8,128]{2,0,1:T(1,128)}), s32[1,8,128]{2,0,1:T(1,128)S(1)}, u32[]{:S(2)}, u32[]{:S(2)}) async-start(s32[1,8,128]{2,0,1:T(1,128)} %bitcast.7), calls=%async_computation.1 | async-start | bytes 8192 | tf_op jit(solution)/shard_map/all_to_all | solution.py:138
  119.7 21.1 %collective-permute-start.7 = (f32[16,2,768]{2,1,0:T(2,128)}, f32[16,2,768]{2,1,0:T(2,128)}, u32[]{:S(2)}, u32[]{:S(2)}) collective-permute-start(f32[16,2,768]{2,1,0:T(2,128)} %get-tuple-element.15), channel_id=1, source_target_pairs={{1,0},{2,1},{3,2},{4,3},{5,4},{6,5},{7,6},{8,7},{9,8},{10,9},{11,1... | collective-permute-start | bytes 294920 | tf_op jit(solution)/shard_map/ppermute | solution.py:18
  119.7 21.1 %collective-permute-start.8 = (f32[16,2,768]{2,1,0:T(2,128)}, f32[16,2,768]{2,1,0:T(2,128)}, u32[]{:S(2)}, u32[]{:S(2)}) collective-permute-start(f32[16,2,768]{2,1,0:T(2,128)} %get-tuple-element.14), channel_id=1, source_target_pairs={{0,1},{1,2},{2,3},{3,4},{4,5},{5,6},{6,7},{7,8},{8,9},{9,10},{10,1... | collective-permute-start | bytes 294920 | tf_op jit(solution)/shard_map/ppermute | solution.py:15
  121.7 19.1 %collective-permute-start.6 = (f32[16,1,768]{2,1,0:T(1,128)}, f32[16,1,768]{2,1,0:T(1,128)S(1)}, u32[]{:S(2)}, u32[]{:S(2)}) collective-permute-start(f32[16,1,768]{2,1,0:T(1,128)} %get-tuple-element.12), channel_id=1, source_target_pairs={{1,0},{2,1},{3,2},{4,3},{5,4},{6,5},{7,6},{8,7},{9,8},{10,9},{11,1... | collective-permute-start | bytes 147464 | tf_op jit(solution)/shard_map/ppermute | solution.py:18
  140.7 1.5 copy-start.3
  144.1 4.7 %collective-permute-start.9 = (f32[16,2,768]{2,1,0:T(2,128)S(1)}, f32[16,2,768]{2,1,0:T(2,128)S(1)}, u32[]{:S(2)}, u32[]{:S(2)}) collective-permute-start(f32[16,2,768]{2,1,0:T(2,128)S(1)} %get-tuple-element.9), channel_id=1, source_target_pairs={{1,0},{2,1},{3,2},{4,3},{5,4},{6,5},{7,6},{8,7},{9,8},{10,9},{11,1... | collective-permute-start | bytes 294920 | tf_op jit(solution)/shard_map/ppermute | solution.py:18
  144.2 8.1 %collective-permute-start.10 = (f32[16,2,768]{2,1,0:T(2,128)S(1)}, f32[16,2,768]{2,1,0:T(2,128)S(1)}, u32[]{:S(2)}, u32[]{:S(2)}) collective-permute-start(f32[16,2,768]{2,1,0:T(2,128)S(1)} %get-tuple-element.8), channel_id=1, source_target_pairs={{0,1},{1,2},{2,3},{3,4},{4,5},{5,6},{6,7},{7,8},{8,9},{9,10},{10,1... | collective-permute-start | bytes 294920 | tf_op jit(solution)/shard_map/ppermute | solution.py:15
